TPU v7x, 256 devices: a whole 4x4x8 slice. The times are simulated.
256 devices in a mesh: lon: 128 (over x, z, y), lat: 2 (over core).
Axes of the slice: x: 4, y: 4, z: 8, core: 2. Of those that a mesh axis runs over, the one named last changes fastest.
Arguments:
- ensemble: float32 [64, 2048, 2048], P(None, 'lon', 'lat'), may hold values from -6 to 6
- obs_lon: int32 [6, 16], replicated, may hold values from 0 to 15
- obs_lat: int32 [6, 16], replicated, may hold values from 0 to 1023
- obs_offset: float32 [6, 2, 16], replicated, may hold values from -0.5 to 0.5
- obs_value: float32 [6, 16], replicated, may hold values from -6 to 6
- obs_error: float32 [6, 16], replicated, may hold values from 0.2 to 2
- owners: int32 [6], replicated, may hold values from 0 to 255
- group_order: int32 [6], replicated, may hold values from 0 to 5, each once
Outputs:
- analysis: float32 [64, 2048, 2048], P(None, 'lon', 'lat')
Inputs may be any that keep to these rules, and one draw needn't show every extreme that they name: `owners`: a tile number: longitude tile index times 2 plus latitude tile index. `group_order`: each group once.
All inputs are finite; a program needn't handle non-finite values.
Results may differ from a plain program's by a relative error of at most 0.00024.
Values sent between devices are 32-bit elements; how exact they have to be, the bound alone decides.
No kernel may reach another device: no remote copies, remote signals or barrier semaphores. Data moves between devices by JAX's collectives and lax.ppermute only.
A program may use at most 64 MiB of HBM per device.

v0:
```python
import functools

import jax
import jax.numpy as jnp
from jax import lax
from jax.experimental import pallas as pl
from jax.experimental.pallas import tpu as pltpu
from jax.sharding import Mesh
from jax.sharding import PartitionSpec as P

LON = ("lon_0", "lon_1", "lon_2")
LANES = 128
STEP = 4
HIGH = lax.Precision.HIGHEST


def priors_kernel(
    sizes, place, lon_in, lat_in, offset_in, owners_in, order_in, field,
    rows_t, lon, lat, offset, owners, order, tile, small_sems, sems
):
    groups, obs, members, lon_cells, lat_cells, lat_tiles = sizes
    my_lon, my_lat = place[0], place[1]
    sources = (owners_in, order_in, lon_in, lat_in, offset_in)
    targets = (owners, order, lon, lat, offset)
    small = [
        pltpu.make_async_copy(source, target, small_sems.at[n])
        for n, (source, target) in enumerate(zip(sources, targets))
    ]
    copies = [
        pltpu.make_async_copy(field.at[:, row, :], tile.at[row], sems.at[row])
        for row in range(lon_cells)
    ]
    for copy in small:
        copy.start()
    rows_t[...] = jnp.zeros_like(rows_t)
    lane = lax.broadcasted_iota(jnp.int32, (1, LANES), 1)
    for copy in small:
        copy.wait()

    def gaps(group):
        owner = owners[group]
        return owner // lat_tiles - my_lon, owner % lat_tiles - my_lat

    def near(group):
        lon_gap, lat_gap = gaps(group)
        return (jnp.abs(lon_gap) <= 1) & (jnp.abs(lat_gap) <= 1)

    touched = near(0)
    for group in range(1, groups):
        touched = touched | near(group)

    @pl.when(touched)
    def _():
        for copy in copies:
            copy.start()
        for copy in copies:
            copy.wait()

    @pl.loop(0, groups)
    def _(turn):
        group = order[turn]
        lon_gap, lat_gap = gaps(group)

        @pl.when(near(group))
        def _():
            @pl.loop(0, obs)
            def _(k):
                p = lon_gap * lon_cells + lon[group, k]
                q = lat_gap * lat_cells + lat[group, k]
                a = offset[group, 0, k]
                b = offset[group, 1, k]
                inside = (p >= -1) & (p <= lon_cells) & (q >= -1) & (q <= lat_cells)

                @pl.when(inside)
                def _():
                    first = jnp.clip(q - 1, 0, lat_cells - 1) // LANES
                    last = jnp.clip(q + 1, 0, lat_cells - 1) // LANES

                    def share(chunk):
                        gap = (lane + chunk * LANES - q).astype(jnp.float32)
                        lat_hat = jnp.maximum(1.0 - jnp.abs(gap - b), 0.0)
                        start = pl.multiple_of(chunk * LANES, LANES)
                        total = jnp.zeros((members, LANES), jnp.float32)
                        for step in (-1, 0, 1):
                            row = p + step
                            hat = jnp.maximum(1.0 - jnp.abs(step - a), 0.0)
                            hat = jnp.where((row >= 0) & (row < lon_cells), hat, 0.0)
                            row = jnp.clip(row, 0, lon_cells - 1)
                            total = total + tile[row, :, pl.ds(start, LANES)] * (lat_hat * hat)
                        found = jnp.sum(total, axis=1, keepdims=True)
                        rows_t[...] += jnp.where(lane == turn * obs + k, found, 0.0)

                    share(first)

                    @pl.when(last != first)
                    def _():
                        share(last)


def table_kernel(
    sizes, value_in, error_in, order_in, field, values, noises, tile, value, error, order, sems,
    tile_sems
):
    groups, obs, members, lon_cells = sizes[:4]
    reads = [
        pltpu.make_async_copy(field.at[:, row, :], tile.at[row], tile_sems.at[row])
        for row in range(lon_cells)
    ]
    copies = [
        pltpu.make_async_copy(source, target, sems.at[n])
        for n, (source, target) in enumerate(
            ((value_in, value), (error_in, error), (order_in, order))
        )
    ]
    for copy in copies + reads:
        copy.start()
    for copy in copies:
        copy.wait()
    for turn in range(groups):
        group = order[turn]
        for k in range(obs):
            row = pl.ds(turn * obs + k, 1)
            values[row, :] = jnp.full((1, LANES), value[group, k], jnp.float32)
            noises[row, :] = jnp.full((1, LANES), error[group, k] * (members - 1.0), jnp.float32)
    for copy in reads:
        copy.wait()


def split(x):
    high = x.astype(jnp.bfloat16)
    return high, (x - high.astype(jnp.float32)).astype(jnp.bfloat16)


def analysis_kernel(
    sizes, rows_t_ref, values, noises, tile, out, done, reduced, spreads, out_sems
):
    groups, obs, members, lon_cells, lat_cells, lat_tiles = sizes
    count = groups * obs
    priors = rows_t_ref[...]
    mean = jnp.mean(priors, axis=0, keepdims=True)
    anomalies = priors - mean
    eye = (
        lax.broadcasted_iota(jnp.int32, (members, LANES), 0)
        == lax.broadcasted_iota(jnp.int32, (members, LANES), 1) % members
    ).astype(jnp.float32)
    both = lax.dot_general(
        anomalies,
        jnp.concatenate([anomalies, eye], axis=1),
        (((0,), (0,)), ((), ())),
        precision=HIGH,
        preferred_element_type=jnp.float32,
    )
    mean_column = jnp.broadcast_to(mean, (LANES, LANES)).T[:count]
    innovation = values[...] - mean_column
    noise = noises[...]
    down = lax.broadcasted_iota(jnp.int32, (count, LANES), 0)
    across = lax.broadcasted_iota(jnp.int32, (count, LANES), 1)
    left_all = both[:count, :LANES] + jnp.where(down == across, noise, 0.0)
    left_all = jnp.where(across == count, innovation, left_all)
    right_all = both[:count, LANES:]

    own = lax.broadcasted_iota(jnp.int32, (obs, LANES), 0)
    half = lax.broadcasted_iota(jnp.int32, (obs, LANES), 1) < members
    for g in range(groups):
        low = g * obs
        tall = 2 * obs if g < groups - 1 else obs
        left = left_all[:tall]
        right = right_all[:tall]
        sub = lax.broadcasted_iota(jnp.int32, (tall, LANES), 0)
        columns = [
            jnp.broadcast_to(left[:, low + i : low + i + 1], (tall, LANES)) for i in range(obs)
        ]
        inverses = jnp.zeros((obs, LANES), jnp.float32)
        shrinks = jnp.zeros((obs, LANES), jnp.float32)
        for j in range(0, obs, 2):
            first, second = columns[j], columns[j + 1]
            corner, cross, other = first[j : j + 1], first[j + 1 : j + 2], second[j + 1 : j + 2]
            inverse = 1.0 / corner
            inverse_next = corner / (corner * other - cross * cross)
            slope = cross * inverse
            shrink = 1.0 / (1.0 + jnp.sqrt(noise[low + j : low + j + 1] * inverse))
            shrink_next = 1.0 / (1.0 + jnp.sqrt(noise[low + j + 1 : low + j + 2] * inverse_next))
            inverses = jnp.where(own == j, inverse, jnp.where(own == j + 1, inverse_next, inverses))
            shrinks = jnp.where(own == j, shrink, jnp.where(own == j + 1, shrink_next, shrinks))
            below = jnp.where(sub > j, first, 0.0)
            below_next = jnp.where(sub > j + 1, second - first * slope, 0.0)

            def eliminate(block, weight, weight_next):
                top, under = block[j : j + 1], block[j + 1 : j + 2]
                scaled = (under - (slope * weight) * top) * (inverse_next * weight_next)
                return block - (below * (top * (inverse * weight)) + below_next * scaled)

            for i in range(j + 2, obs):
                columns[i] = eliminate(columns[i], 1.0, 1.0)
            left = eliminate(left, 1.0, 1.0)
            right = eliminate(
                right, jnp.where(half[0:1], 1.0, shrink), jnp.where(half[0:1], 1.0, shrink_next)
            )
        following = (left[obs:], right[obs:])
        left, right = left[:obs], right[:obs]
        innovations = jnp.broadcast_to(left[:, count : count + 1], (obs, LANES))
        spreads[low : low + obs, :] = inverses * (innovations - shrinks * right)
        right = right * jnp.where(half, 1.0, shrinks)
        reduced[low : low + obs, :] = right
        if g == groups - 2:
            left_all, right_all = following
        elif g < groups - 2:
            change = jnp.dot(
                (left * inverses).T[low + 2 * obs : count],
                jnp.concatenate([left, right], axis=1),
                precision=HIGH,
                preferred_element_type=jnp.float32,
            )
            left_all = jnp.concatenate(
                [following[0], left_all[2 * obs :] - change[:, :LANES]], axis=0
            )
            right_all = jnp.concatenate(
                [following[1], right_all[2 * obs :] - change[:, LANES:]], axis=0
            )

    change = lax.dot_general(
        spreads[...],
        reduced[...],
        (((0,), (0,)), ((), ())),
        precision=HIGH,
        preferred_element_type=jnp.float32,
    )[members : 2 * members, :members]
    high, low_part = split(change)
    weights = jnp.concatenate([high, high, low_part], axis=1)

    @pl.loop(0, lat_cells // LANES)
    def _(c):
        lanes = pl.ds(pl.multiple_of(c * LANES, LANES), LANES)
        for part in range(lon_cells // STEP):
            rows = range(part * STEP, (part + 1) * STEP)
            block = jnp.concatenate([tile[row, :, lanes] for row in rows], axis=1)
            top, rest = split(block)
            new = block + jnp.dot(
                weights,
                jnp.concatenate([top, rest, top], axis=0),
                preferred_element_type=jnp.float32,
            )
            for n, row in enumerate(rows):
                done[c, pl.ds(row, members, stride=lon_cells), :] = new[
                    :, n * LANES : (n + 1) * LANES
                ]
        pltpu.make_async_copy(done.at[c], out.at[:, lanes], out_sems.at[c]).start()

    for c in range(lat_cells // LANES):
        pltpu.make_async_copy(
            done.at[c], out.at[:, pl.ds(c * LANES, LANES)], out_sems.at[c]
        ).wait()


def pairwise_sum(shard, axis, partners):
    size = lax.axis_size(axis)
    arrived = [
        lax.ppermute(shard, axis, [(i, partner(i)) for i in range(size)]) for partner in partners
    ]
    for piece in arrived:
        shard = shard + piece
    return shard


def total_over_tiles(shard):
    quad = (lambda i: i ^ 1, lambda i: i ^ 2, lambda i: i ^ 3)
    shard = pairwise_sum(shard, "lat", (lambda i: i ^ 1,))
    shard = pairwise_sum(shard, "lon_0", quad)
    shard = pairwise_sum(shard, "lon_2", quad)
    shard = pairwise_sum(shard, "lon_1", (lambda i: 7 - i,))
    return pairwise_sum(shard, "lon_1", quad)


def body(ensemble, obs_lon, obs_lat, obs_offset, obs_value, obs_error, owners, group_order):
    members, lon_cells, lat_cells = ensemble.shape
    groups, obs = obs_lon.shape
    sizes = (groups, obs, members, lon_cells, lat_cells, lax.axis_size("lat"))
    count = groups * obs
    place = jnp.stack([lax.axis_index(LON), lax.axis_index("lat")]).astype(jnp.int32)
    smem = pl.BlockSpec(memory_space=pltpu.SMEM)
    vmem = pl.BlockSpec(memory_space=pltpu.VMEM)
    hbm = pl.BlockSpec(memory_space=pltpu.HBM)
    tile_shape = (lon_cells, members, lat_cells)
    field, lon, lat, offset, value, error, owner, order = (
        pltpu.with_memory_space_constraint(array, pltpu.HBM)
        for array in (
            ensemble, obs_lon, obs_lat, obs_offset, obs_value, obs_error, owners, group_order
        )
    )
    rows_t = pl.pallas_call(
        functools.partial(priors_kernel, sizes),
        out_shape=jax.ShapeDtypeStruct((members, LANES), jnp.float32),
        in_specs=[smem] + [hbm] * 6,
        out_specs=vmem,
        scratch_shapes=[
            pltpu.SMEM(obs_lon.shape, jnp.int32),
            pltpu.SMEM(obs_lat.shape, jnp.int32),
            pltpu.SMEM(obs_offset.shape, jnp.float32),
            pltpu.SMEM(owners.shape, jnp.int32),
            pltpu.SMEM(group_order.shape, jnp.int32),
            pltpu.VMEM(tile_shape, jnp.float32),
            pltpu.SemaphoreType.DMA((5,)),
            pltpu.SemaphoreType.DMA((lon_cells,)),
        ],
        compiler_params=pltpu.CompilerParams(vmem_limit_bytes=10 << 20),
        name="priors",
    )(place, lon, lat, offset, owner, order, field)
    values, noises, tile = pl.pallas_call(
        functools.partial(table_kernel, sizes),
        out_shape=(
            jax.ShapeDtypeStruct((count, LANES), jnp.float32),
            jax.ShapeDtypeStruct((count, LANES), jnp.float32),
            jax.ShapeDtypeStruct(tile_shape, jnp.float32),
        ),
        in_specs=[hbm] * 4,
        out_specs=(vmem,) * 3,
        scratch_shapes=[
            pltpu.SMEM(obs_value.shape, jnp.float32),
            pltpu.SMEM(obs_error.shape, jnp.float32),
            pltpu.SMEM(group_order.shape, jnp.int32),
            pltpu.SemaphoreType.DMA((3,)),
            pltpu.SemaphoreType.DMA((lon_cells,)),
        ],
        compiler_params=pltpu.CompilerParams(vmem_limit_bytes=6 << 20),
        cost_estimate=pl.CostEstimate(flops=1 << 20, bytes_accessed=4 << 20, transcendentals=0),
        name="tables",
    )(value, error, order, field)
    rows_t = total_over_tiles(rows_t)
    return pl.pallas_call(
        functools.partial(analysis_kernel, sizes),
        out_shape=jax.ShapeDtypeStruct((members * lon_cells, lat_cells), jnp.float32),
        in_specs=[vmem] * 4,
        out_specs=hbm,
        scratch_shapes=[
            pltpu.VMEM((lat_cells // LANES, members * lon_cells, LANES), jnp.float32),
            pltpu.VMEM((count, LANES), jnp.float32),
            pltpu.VMEM((count, LANES), jnp.float32),
            pltpu.SemaphoreType.DMA((lat_cells // LANES,)),
        ],
        compiler_params=pltpu.CompilerParams(vmem_limit_bytes=16 << 20),
        name="analysis",
    )(rows_t, values, noises, tile).reshape(ensemble.shape)


def solution(mesh):
    torus = Mesh(
        mesh.devices.reshape(4, 8, 4, mesh.shape["lat"]), ("lon_0", "lon_1", "lon_2", "lat")
    )
    in_specs = (P(None, LON, "lat"), P(), P(), P(), P(), P(), P(), P())
    out_specs = P(None, LON, "lat")
    return jax.shard_map(body, mesh=torus, in_specs=in_specs, out_specs=out_specs, check_vma=False)
```

profile of v0, /device:TPU:32, one launch (start us, length us, event | category | flops | bytes accessed | tf_op | source)
XLA Modules:
  0.0 44.3 jit_solution(1768230940688835894)
XLA Ops:
  0.0 0.1 pad_add_fusion.place
  0.1 1.8 %priors.1 = f32[64,128]{1,0:T(8,128)S(1)} custom-call(s32[2]{0:T(128)S(1)} %pad_add_fusion.place, s32[6,16]{1,0:T(8,128)} %lon_in.1, s32[6,16]{1,0:T(8,128)} %lat_in.1, f32[6,2,16]{2,1,0:T(2,128)} %offset_in.1, s32[6]{0:T(128)} %owners_in.1, s32[6]{0:T(128)} %order_in.3, f32[64,16,1024]{2,1,0:T(8,128)} %field.3), custom_call_target="tpu_custom_call" | custom-call | tf_op jit(solution)/shard_map/priors/pallas_call | solution.py:290
  1.9 0.1 collective-permute-start
  2.0 1.2 %collective-permute-done = f32[64,128]{1,0:T(8,128)S(1)} collective-permute-done((f32[64,128]{1,0:T(8,128)S(1)}, f32[64,128]{1,0:T(8,128)S(1)}, u32[]{:S(2)}, u32[]{:S(2)}) %collective-permute-start) | collective-permute-done | bytes 32800 | tf_op jit(solution)/shard_map/ppermute | solution.py:258
  3.2 2.8 %collective-permute-start.3 = (f32[64,128]{1,0:T(8,128)S(1)}, f32[64,128]{1,0:T(8,128)S(1)}, u32[]{:S(2)}, u32[]{:S(2)}) collective-permute-start(f32[64,128]{1,0:T(8,128)S(1)} %add.41), channel_id=1, source_target_pairs={{0,192},{64,128},{128,64},{192,0},{1,193},{65,129},{129,65},{193,1... | collective-permute-start | bytes 98312 | tf_op jit(solution)/shard_map/ppermute | solution.py:258
  6.0 0.8 %collective-permute-start.2 = (f32[64,128]{1,0:T(8,128)S(1)}, f32[64,128]{1,0:T(8,128)S(1)}, u32[]{:S(2)}, u32[]{:S(2)}) collective-permute-start(f32[64,128]{1,0:T(8,128)S(1)} %add.41), channel_id=1, source_target_pairs={{0,128},{64,192},{128,0},{192,64},{1,129},{65,193},{129,1},{193,65... | collective-permute-start | bytes 98312 | tf_op jit(solution)/shard_map/ppermute | solution.py:258
  6.8 0.5 %collective-permute-start.1 = (f32[64,128]{1,0:T(8,128)S(1)}, f32[64,128]{1,0:T(8,128)S(1)}, u32[]{:S(2)}, u32[]{:S(2)}) collective-permute-start(f32[64,128]{1,0:T(8,128)S(1)} %add.41), channel_id=1, source_target_pairs={{0,64},{64,0},{128,192},{192,128},{1,65},{65,1},{129,193},{193,129... | collective-permute-start | bytes 98312 | tf_op jit(solution)/shard_map/ppermute | solution.py:258
  7.3 1.0 %collective-permute-done.3 = f32[64,128]{1,0:T(8,128)S(1)} collective-permute-done((f32[64,128]{1,0:T(8,128)S(1)}, f32[64,128]{1,0:T(8,128)S(1)}, u32[]{:S(2)}, u32[]{:S(2)}) %collective-permute-start.3) | collective-permute-done | bytes 32800 | tf_op jit(solution)/shard_map/ppermute | solution.py:258
  8.3 3.1 %collective-permute-done.2 = f32[64,128]{1,0:T(8,128)S(1)} collective-permute-done((f32[64,128]{1,0:T(8,128)S(1)}, f32[64,128]{1,0:T(8,128)S(1)}, u32[]{:S(2)}, u32[]{:S(2)}) %collective-permute-start.2) | collective-permute-done | bytes 32800 | tf_op jit(solution)/shard_map/ppermute | solution.py:258
  11.4 3.1 %collective-permute-start.6 = (f32[64,128]{1,0:T(8,128)S(1)}, f32[64,128]{1,0:T(8,128)S(1)}, u32[]{:S(2)}, u32[]{:S(2)}) collective-permute-start(f32[64,128]{1,0:T(8,128)S(1)} %add_add_fusion.2), channel_id=1, source_target_pairs={{0,6},{2,4},{4,2},{6,0},{1,7},{3,5},{5,3},{7,1},{8,14},{10,12},{12... | collective-permute-start | bytes 98312 | tf_op jit(solution)/shard_map/ppermute | solution.py:258
  14.5 0.6 %collective-permute-start.5 = (f32[64,128]{1,0:T(8,128)S(1)}, f32[64,128]{1,0:T(8,128)S(1)}, u32[]{:S(2)}, u32[]{:S(2)}) collective-permute-start(f32[64,128]{1,0:T(8,128)S(1)} %add_add_fusion.2), channel_id=1, source_target_pairs={{0,4},{2,6},{4,0},{6,2},{1,5},{3,7},{5,1},{7,3},{8,12},{10,14},{12... | collective-permute-start | bytes 98312 | tf_op jit(solution)/shard_map/ppermute | solution.py:258
  15.1 0.5 %collective-permute-start.4 = (f32[64,128]{1,0:T(8,128)S(1)}, f32[64,128]{1,0:T(8,128)S(1)}, u32[]{:S(2)}, u32[]{:S(2)}) collective-permute-start(f32[64,128]{1,0:T(8,128)S(1)} %add_add_fusion.2), channel_id=1, source_target_pairs={{0,2},{2,0},{4,6},{6,4},{1,3},{3,1},{5,7},{7,5},{8,10},{10,8},{12,... | collective-permute-start | bytes 98312 | tf_op jit(solution)/shard_map/ppermute | solution.py:258
  15.6 1.0 %collective-permute-done.6 = f32[64,128]{1,0:T(8,128)S(1)} collective-permute-done((f32[64,128]{1,0:T(8,128)S(1)}, f32[64,128]{1,0:T(8,128)S(1)}, u32[]{:S(2)}, u32[]{:S(2)}) %collective-permute-start.6) | collective-permute-done | bytes 32800 | tf_op jit(solution)/shard_map/ppermute | solution.py:258
  16.6 3.3 %collective-permute-done.5 = f32[64,128]{1,0:T(8,128)S(1)} collective-permute-done((f32[64,128]{1,0:T(8,128)S(1)}, f32[64,128]{1,0:T(8,128)S(1)}, u32[]{:S(2)}, u32[]{:S(2)}) %collective-permute-start.5) | collective-permute-done | bytes 32800 | tf_op jit(solution)/shard_map/ppermute | solution.py:258
  19.9 0.0 collective-permute-done.4
  19.9 7.3 %collective-permute-start.7 = (f32[64,128]{1,0:T(8,128)S(1)}, f32[64,128]{1,0:T(8,128)S(1)}, u32[]{:S(2)}, u32[]{:S(2)}) collective-permute-start(f32[64,128]{1,0:T(8,128)S(1)} %add_add_fusion.1), channel_id=1, source_target_pairs={{0,56},{8,48},{16,40},{24,32},{32,24},{40,16},{48,8},{56,0},{1,57}... | collective-permute-start | bytes 98312 | tf_op jit(solution)/shard_map/ppermute | solution.py:258
  27.2 1.9 %collective-permute-done.7 = f32[64,128]{1,0:T(8,128)S(1)} collective-permute-done((f32[64,128]{1,0:T(8,128)S(1)}, f32[64,128]{1,0:T(8,128)S(1)}, u32[]{:S(2)}, u32[]{:S(2)}) %collective-permute-start.7) | collective-permute-done | bytes 32800 | tf_op jit(solution)/shard_map/ppermute | solution.py:258
  29.1 1.8 %collective-permute-start.10 = (f32[64,128]{1,0:T(8,128)S(1)}, f32[64,128]{1,0:T(8,128)S(1)}, u32[]{:S(2)}, u32[]{:S(2)}) collective-permute-start(f32[64,128]{1,0:T(8,128)S(1)} %add.48), channel_id=1, source_target_pairs={{0,24},{8,16},{16,8},{24,0},{32,56},{40,48},{48,40},{56,32},{1,25}... | collective-permute-start | bytes 98312 | tf_op jit(solution)/shard_map/ppermute | solution.py:258
  30.9 2.9 %collective-permute-start.9 = (f32[64,128]{1,0:T(8,128)S(1)}, f32[64,128]{1,0:T(8,128)S(1)}, u32[]{:S(2)}, u32[]{:S(2)}) collective-permute-start(f32[64,128]{1,0:T(8,128)S(1)} %add.48), channel_id=1, source_target_pairs={{0,16},{8,24},{16,0},{24,8},{32,48},{40,56},{48,32},{56,40},{1,17}... | collective-permute-start | bytes 98312 | tf_op jit(solution)/shard_map/ppermute | solution.py:258
  33.8 2.6 %tables.1 = (f32[96,128]{1,0:T(8,128)S(1)}, f32[96,128]{1,0:T(8,128)S(1)}, f32[16,64,1024]{2,1,0:T(8,128)S(1)}) custom-call(f32[6,16]{1,0:T(8,128)} %value_in.1, f32[6,16]{1,0:T(8,128)} %error_in.1, s32[6]{0:T(128)} %order_in.3, f32[64,16,1024]{2,1,0:T(8,128)} %field.3), custom_call_target="tpu_custom_call" | custom-call | flops 1048576 | bytes 4194304 | tf_op jit(solution)/shard_map/tables/pallas_call | solution.py:308
  36.4 0.0 collective-permute-done.10
  36.4 0.0 collective-permute-done.9
  36.4 1.3 %collective-permute-done.8 = f32[64,128]{1,0:T(8,128)S(1)} collective-permute-done((f32[64,128]{1,0:T(8,128)S(1)}, f32[64,128]{1,0:T(8,128)S(1)}, u32[]{:S(2)}, u32[]{:S(2)}) %collective-permute-start.8) | collective-permute-done | bytes 32800 | tf_op jit(solution)/shard_map/ppermute | solution.py:258
  37.7 6.6 %analysis.1 = f32[1024,1024]{1,0:T(8,128)} custom-call(f32[64,128]{1,0:T(8,128)S(1)} %add_add_fusion.rows_t_ref, f32[96,128]{1,0:T(8,128)S(1)} %get-tuple-element.8.values, f32[96,128]{1,0:T(8,128)S(1)} %get-tuple-element.9.noises, f32[16,64,1024]{2,1,0:T(8,128)S(1)} %get-tuple-element.10.tile), custom_call_target="tpu_custom_call" | custom-call | tf_op jit(solution)/shard_map/analysis/pallas_call | solution.py:329
  (7 shorter events, 0.0 us)
Async XLA Ops:
  1.9 1.3 %collective-permute-start = (f32[64,128]{1,0:T(8,128)S(1)}, f32[64,128]{1,0:T(8,128)S(1)}, u32[]{:S(2)}, u32[]{:S(2)}) collective-permute-start(f32[64,128]{1,0:T(8,128)S(1)} %priors.1), channel_id=1, source_target_pairs={{0,1},{1,0},{2,3},{3,2},{4,5},{5,4},{6,7},{7,6},{8,9},{9,8},{10,11... | collective-permute-start | bytes 98312 | tf_op jit(solution)/shard_map/ppermute | solution.py:258
  3.2 5.1 %collective-permute-start.3 = (f32[64,128]{1,0:T(8,128)S(1)}, f32[64,128]{1,0:T(8,128)S(1)}, u32[]{:S(2)}, u32[]{:S(2)}) collective-permute-start(f32[64,128]{1,0:T(8,128)S(1)} %add.41), channel_id=1, source_target_pairs={{0,192},{64,128},{128,64},{192,0},{1,193},{65,129},{129,65},{193,1... | collective-permute-start | bytes 98312 | tf_op jit(solution)/shard_map/ppermute | solution.py:258
  6.0 5.4 %collective-permute-start.2 = (f32[64,128]{1,0:T(8,128)S(1)}, f32[64,128]{1,0:T(8,128)S(1)}, u32[]{:S(2)}, u32[]{:S(2)}) collective-permute-start(f32[64,128]{1,0:T(8,128)S(1)} %add.41), channel_id=1, source_target_pairs={{0,128},{64,192},{128,0},{192,64},{1,129},{65,193},{129,1},{193,65... | collective-permute-start | bytes 98312 | tf_op jit(solution)/shard_map/ppermute | solution.py:258
  6.8 4.6 %collective-permute-start.1 = (f32[64,128]{1,0:T(8,128)S(1)}, f32[64,128]{1,0:T(8,128)S(1)}, u32[]{:S(2)}, u32[]{:S(2)}) collective-permute-start(f32[64,128]{1,0:T(8,128)S(1)} %add.41), channel_id=1, source_target_pairs={{0,64},{64,0},{128,192},{192,128},{1,65},{65,1},{129,193},{193,129... | collective-permute-start | bytes 98312 | tf_op jit(solution)/shard_map/ppermute | solution.py:258
  11.4 5.2 %collective-permute-start.6 = (f32[64,128]{1,0:T(8,128)S(1)}, f32[64,128]{1,0:T(8,128)S(1)}, u32[]{:S(2)}, u32[]{:S(2)}) collective-permute-start(f32[64,128]{1,0:T(8,128)S(1)} %add_add_fusion.2), channel_id=1, source_target_pairs={{0,6},{2,4},{4,2},{6,0},{1,7},{3,5},{5,3},{7,1},{8,14},{10,12},{12... | collective-permute-start | bytes 98312 | tf_op jit(solution)/shard_map/ppermute | solution.py:258
  14.5 5.4 %collective-permute-start.5 = (f32[64,128]{1,0:T(8,128)S(1)}, f32[64,128]{1,0:T(8,128)S(1)}, u32[]{:S(2)}, u32[]{:S(2)}) collective-permute-start(f32[64,128]{1,0:T(8,128)S(1)} %add_add_fusion.2), channel_id=1, source_target_pairs={{0,4},{2,6},{4,0},{6,2},{1,5},{3,7},{5,1},{7,3},{8,12},{10,14},{12... | collective-permute-start | bytes 98312 | tf_op jit(solution)/shard_map/ppermute | solution.py:258
  15.1 4.8 %collective-permute-start.4 = (f32[64,128]{1,0:T(8,128)S(1)}, f32[64,128]{1,0:T(8,128)S(1)}, u32[]{:S(2)}, u32[]{:S(2)}) collective-permute-start(f32[64,128]{1,0:T(8,128)S(1)} %add_add_fusion.2), channel_id=1, source_target_pairs={{0,2},{2,0},{4,6},{6,4},{1,3},{3,1},{5,7},{7,5},{8,10},{10,8},{12,... | collective-permute-start | bytes 98312 | tf_op jit(solution)/shard_map/ppermute | solution.py:258
  19.9 9.2 %collective-permute-start.7 = (f32[64,128]{1,0:T(8,128)S(1)}, f32[64,128]{1,0:T(8,128)S(1)}, u32[]{:S(2)}, u32[]{:S(2)}) collective-permute-start(f32[64,128]{1,0:T(8,128)S(1)} %add_add_fusion.1), channel_id=1, source_target_pairs={{0,56},{8,48},{16,40},{24,32},{32,24},{40,16},{48,8},{56,0},{1,57}... | collective-permute-start | bytes 98312 | tf_op jit(solution)/shard_map/ppermute | solution.py:258
  29.1 7.3 %collective-permute-start.10 = (f32[64,128]{1,0:T(8,128)S(1)}, f32[64,128]{1,0:T(8,128)S(1)}, u32[]{:S(2)}, u32[]{:S(2)}) collective-permute-start(f32[64,128]{1,0:T(8,128)S(1)} %add.48), channel_id=1, source_target_pairs={{0,24},{8,16},{16,8},{24,0},{32,56},{40,48},{48,40},{56,32},{1,25}... | collective-permute-start | bytes 98312 | tf_op jit(solution)/shard_map/ppermute | solution.py:258
  30.9 5.5 %collective-permute-start.9 = (f32[64,128]{1,0:T(8,128)S(1)}, f32[64,128]{1,0:T(8,128)S(1)}, u32[]{:S(2)}, u32[]{:S(2)}) collective-permute-start(f32[64,128]{1,0:T(8,128)S(1)} %add.48), channel_id=1, source_target_pairs={{0,16},{8,24},{16,0},{24,8},{32,48},{40,56},{48,32},{56,40},{1,17}... | collective-permute-start | bytes 98312 | tf_op jit(solution)/shard_map/ppermute | solution.py:258
  33.8 3.9 %collective-permute-start.8 = (f32[64,128]{1,0:T(8,128)S(1)}, f32[64,128]{1,0:T(8,128)S(1)}, u32[]{:S(2)}, u32[]{:S(2)}) collective-permute-start(f32[64,128]{1,0:T(8,128)S(1)} %add.48), channel_id=1, source_target_pairs={{0,8},{8,0},{16,24},{24,16},{32,40},{40,32},{48,56},{56,48},{1,9},... | collective-permute-start | bytes 98312 | tf_op jit(solution)/shard_map/ppermute | solution.py:258
where the time goes:
time: 44.4 us; the launch traced here: 44.3 us
  starting transfers between devices  20.3 us (46%)
  waiting for transfers between devices  12.8 us (29%)
  Pallas kernels  11 us (25%)
    ppermute x11, starting transfers between devices, pairwise_sum(): lax.ppermute(shard, axis, [(i, partner(i)) for i in range(size)])  20.3 us
    ppermute x11, waiting for transfers between devices, pairwise_sum(): lax.ppermute(shard, axis, [(i, partner(i)) for i in range(size)])  12.8 us
    pallas_call x1, Pallas kernels, body(): pl.pallas_call(functools.partial(analysis_kernel, sizes), out_shape=jax.S...  6.55 us
    pallas_call x1, Pallas kernels, body(): pl.pallas_call(functools.partial(table_kernel, sizes), out_shape=(jax.Sha...  2.59 us
    pallas_call x1, Pallas kernels, body(): pl.pallas_call(functools.partial(priors_kernel, sizes), out_shape=jax.Sha...  1.81 us
  transfers between devices with their start and end apart: 11, of which 7 were waited for; matrix products, arithmetic and copies ran while one was open for 0% of the time, Pallas kernels for 6%

commit v1 on v0

--- a/solution.py
+++ b/solution.py
@@ -16,7 +16,7 @@
 
 def priors_kernel(
     sizes, place, lon_in, lat_in, offset_in, owners_in, order_in, field,
-    rows_t, lon, lat, offset, owners, order, tile, small_sems, sems
+    rows_t, tile, lon, lat, offset, owners, order, small_sems, sems
 ):
     groups, obs, members, lon_cells, lat_cells, lat_tiles = sizes
     my_lon, my_lat = place[0], place[1]
@@ -30,11 +30,11 @@
         pltpu.make_async_copy(field.at[:, row, :], tile.at[row], sems.at[row])
         for row in range(lon_cells)
     ]
-    for copy in small:
+    for copy in small + copies:
         copy.start()
     rows_t[...] = jnp.zeros_like(rows_t)
     lane = lax.broadcasted_iota(jnp.int32, (1, LANES), 1)
-    for copy in small:
+    for copy in small + copies:
         copy.wait()
 
     def gaps(group):
@@ -44,17 +44,6 @@
     def near(group):
         lon_gap, lat_gap = gaps(group)
         return (jnp.abs(lon_gap) <= 1) & (jnp.abs(lat_gap) <= 1)
-
-    touched = near(0)
-    for group in range(1, groups):
-        touched = touched | near(group)
-
-    @pl.when(touched)
-    def _():
-        for copy in copies:
-            copy.start()
-        for copy in copies:
-            copy.wait()
 
     @pl.loop(0, groups)
     def _(turn):
@@ -97,22 +86,15 @@
                         share(last)
 
 
-def table_kernel(
-    sizes, value_in, error_in, order_in, field, values, noises, tile, value, error, order, sems,
-    tile_sems
-):
-    groups, obs, members, lon_cells = sizes[:4]
-    reads = [
-        pltpu.make_async_copy(field.at[:, row, :], tile.at[row], tile_sems.at[row])
-        for row in range(lon_cells)
-    ]
+def table_kernel(sizes, value_in, error_in, order_in, values, noises, value, error, order, sems):
+    groups, obs, members = sizes[:3]
     copies = [
         pltpu.make_async_copy(source, target, sems.at[n])
         for n, (source, target) in enumerate(
             ((value_in, value), (error_in, error), (order_in, order))
         )
     ]
-    for copy in copies + reads:
+    for copy in copies:
         copy.start()
     for copy in copies:
         copy.wait()
@@ -122,8 +104,6 @@
             row = pl.ds(turn * obs + k, 1)
             values[row, :] = jnp.full((1, LANES), value[group, k], jnp.float32)
             noises[row, :] = jnp.full((1, LANES), error[group, k] * (members - 1.0), jnp.float32)
-    for copy in reads:
-        copy.wait()
 
 
 def split(x):
@@ -287,44 +267,41 @@
             ensemble, obs_lon, obs_lat, obs_offset, obs_value, obs_error, owners, group_order
         )
     )
-    rows_t = pl.pallas_call(
+    rows_t, tile = pl.pallas_call(
         functools.partial(priors_kernel, sizes),
-        out_shape=jax.ShapeDtypeStruct((members, LANES), jnp.float32),
+        out_shape=(
+            jax.ShapeDtypeStruct((members, LANES), jnp.float32),
+            jax.ShapeDtypeStruct(tile_shape, jnp.float32),
+        ),
         in_specs=[smem] + [hbm] * 6,
-        out_specs=vmem,
+        out_specs=(vmem, vmem),
         scratch_shapes=[
             pltpu.SMEM(obs_lon.shape, jnp.int32),
             pltpu.SMEM(obs_lat.shape, jnp.int32),
             pltpu.SMEM(obs_offset.shape, jnp.float32),
             pltpu.SMEM(owners.shape, jnp.int32),
             pltpu.SMEM(group_order.shape, jnp.int32),
-            pltpu.VMEM(tile_shape, jnp.float32),
             pltpu.SemaphoreType.DMA((5,)),
             pltpu.SemaphoreType.DMA((lon_cells,)),
         ],
         compiler_params=pltpu.CompilerParams(vmem_limit_bytes=10 << 20),
         name="priors",
     )(place, lon, lat, offset, owner, order, field)
-    values, noises, tile = pl.pallas_call(
+    values, noises = pl.pallas_call(
         functools.partial(table_kernel, sizes),
-        out_shape=(
-            jax.ShapeDtypeStruct((count, LANES), jnp.float32),
-            jax.ShapeDtypeStruct((count, LANES), jnp.float32),
-            jax.ShapeDtypeStruct(tile_shape, jnp.float32),
-        ),
-        in_specs=[hbm] * 4,
-        out_specs=(vmem,) * 3,
+        out_shape=(jax.ShapeDtypeStruct((count, LANES), jnp.float32),) * 2,
+        in_specs=[hbm] * 3,
+        out_specs=(vmem, vmem),
         scratch_shapes=[
             pltpu.SMEM(obs_value.shape, jnp.float32),
             pltpu.SMEM(obs_error.shape, jnp.float32),
             pltpu.SMEM(group_order.shape, jnp.int32),
             pltpu.SemaphoreType.DMA((3,)),
-            pltpu.SemaphoreType.DMA((lon_cells,)),
         ],
-        compiler_params=pltpu.CompilerParams(vmem_limit_bytes=6 << 20),
+        compiler_params=pltpu.CompilerParams(vmem_limit_bytes=1 << 20),
         cost_estimate=pl.CostEstimate(flops=1 << 20, bytes_accessed=4 << 20, transcendentals=0),
         name="tables",
-    )(value, error, order, field)
+    )(value, error, order)
     rows_t = total_over_tiles(rows_t)
     return pl.pallas_call(
         functools.partial(analysis_kernel, sizes),

time: 44.4 us -> 43.3 us (0.975)
  starting transfers between devices: 20.3 us -> 18.3 us
  waiting for transfers between devices: 12.8 us -> 14.1 us
    ppermute x11, starting transfers between devices: 20.3 us -> 18.3 us  [pairwise_sum(): lax.ppermute(shard, axis, [(i, partner(i)) for i in range(size)])]
    pallas_call x1, Pallas kernels: 2.59 us -> 0.9 us  [body(): pl.pallas_call(functools.partial(table_kernel, sizes), out_shape=(jax.Sha...]
    pallas_call x1, Pallas kernels: 1.81 us -> 3.17 us  [body(): pl.pallas_call(functools.partial(priors_kernel, sizes), out_shape=(jax.Sh...]
    ppermute x11, waiting for transfers between devices: 12.8 us -> 14.1 us  [pairwise_sum(): lax.ppermute(shard, axis, [(i, partner(i)) for i in range(size)])]
  transfers between devices with their start and end apart: 11 -> 11, of which waited for: 7 -> 8; matrix products, arithmetic and copies ran while one was open for 0% -> 0% of each run, Pallas kernels for 6% -> 2%
where the time goes in v1:
time: 43.3 us; the launch traced here: 43.2 us
  starting transfers between devices  18.3 us (42%)
  waiting for transfers between devices  14.1 us (33%)
  Pallas kernels  10.6 us (24%)
    ppermute x11, starting transfers between devices, pairwise_sum(): lax.ppermute(shard, axis, [(i, partner(i)) for i in range(size)])  18.3 us
    ppermute x11, waiting for transfers between devices, pairwise_sum(): lax.ppermute(shard, axis, [(i, partner(i)) for i in range(size)])  14.1 us
    pallas_call x1, Pallas kernels, body(): pl.pallas_call(functools.partial(analysis_kernel, sizes), out_shape=jax.S...  6.55 us
    pallas_call x1, Pallas kernels, body(): pl.pallas_call(functools.partial(priors_kernel, sizes), out_shape=(jax.Sh...  3.17 us
    pallas_call x1, Pallas kernels, body(): pl.pallas_call(functools.partial(table_kernel, sizes), out_shape=(jax.Sha...  0.9 us
  transfers between devices with their start and end apart: 11, of which 8 were waited for; matrix products, arithmetic and copies ran while one was open for 0% of the time, Pallas kernels for 2%

profile of v1, /device:TPU:32, one launch (start us, length us, event | category | flops | bytes accessed | tf_op | source)
XLA Modules:
  0.0 43.2 jit_solution(15697218569413980375)
XLA Ops:
  0.0 0.1 pad_add_fusion.place
  0.1 3.2 %priors.1 = (f32[64,128]{1,0:T(8,128)S(1)}, f32[16,64,1024]{2,1,0:T(8,128)S(1)}) custom-call(s32[2]{0:T(128)S(1)} %pad_add_fusion.place, s32[6,16]{1,0:T(8,128)} %lon_in.1, s32[6,16]{1,0:T(8,128)} %lat_in.1, f32[6,2,16]{2,1,0:T(2,128)} %offset_in.1, s32[6]{0:T(128)} %owners_in.1, s32[6]{0:T(128)} %order_in.3, f32[64,16,1024]{2,1,0:T(8,128)} %field.1), custom_call_target="tpu_custom_call" | custom-call | tf_op jit(solution)/shard_map/priors/pallas_call | solution.py:270
  3.2 0.1 collective-permute-start
  3.4 1.2 %collective-permute-done = f32[64,128]{1,0:T(8,128)S(1)} collective-permute-done((f32[64,128]{1,0:T(8,128)S(1)}, f32[64,128]{1,0:T(8,128)S(1)}, u32[]{:S(2)}, u32[]{:S(2)}) %collective-permute-start) | collective-permute-done | bytes 32800 | tf_op jit(solution)/shard_map/ppermute | solution.py:238
  4.6 2.8 %collective-permute-start.3 = (f32[64,128]{1,0:T(8,128)S(1)}, f32[64,128]{1,0:T(8,128)S(1)}, u32[]{:S(2)}, u32[]{:S(2)}) collective-permute-start(f32[64,128]{1,0:T(8,128)S(1)} %add.41), channel_id=1, source_target_pairs={{0,192},{64,128},{128,64},{192,0},{1,193},{65,129},{129,65},{193,1... | collective-permute-start | bytes 98312 | tf_op jit(solution)/shard_map/ppermute | solution.py:238
  7.3 1.0 %collective-permute-start.2 = (f32[64,128]{1,0:T(8,128)S(1)}, f32[64,128]{1,0:T(8,128)S(1)}, u32[]{:S(2)}, u32[]{:S(2)}) collective-permute-start(f32[64,128]{1,0:T(8,128)S(1)} %add.41), channel_id=1, source_target_pairs={{0,128},{64,192},{128,0},{192,64},{1,129},{65,193},{129,1},{193,65... | collective-permute-start | bytes 98312 | tf_op jit(solution)/shard_map/ppermute | solution.py:238
  8.3 0.4 collective-permute-start.1
  8.6 1.0 %collective-permute-done.3 = f32[64,128]{1,0:T(8,128)S(1)} collective-permute-done((f32[64,128]{1,0:T(8,128)S(1)}, f32[64,128]{1,0:T(8,128)S(1)}, u32[]{:S(2)}, u32[]{:S(2)}) %collective-permute-start.3) | collective-permute-done | bytes 32800 | tf_op jit(solution)/shard_map/ppermute | solution.py:238
  9.7 3.1 %collective-permute-done.2 = f32[64,128]{1,0:T(8,128)S(1)} collective-permute-done((f32[64,128]{1,0:T(8,128)S(1)}, f32[64,128]{1,0:T(8,128)S(1)}, u32[]{:S(2)}, u32[]{:S(2)}) %collective-permute-start.2) | collective-permute-done | bytes 32800 | tf_op jit(solution)/shard_map/ppermute | solution.py:238
  12.7 0.0 collective-permute-done.1
  12.7 3.1 %collective-permute-start.6 = (f32[64,128]{1,0:T(8,128)S(1)}, f32[64,128]{1,0:T(8,128)S(1)}, u32[]{:S(2)}, u32[]{:S(2)}) collective-permute-start(f32[64,128]{1,0:T(8,128)S(1)} %add_add_fusion.2), channel_id=1, source_target_pairs={{0,6},{2,4},{4,2},{6,0},{1,7},{3,5},{5,3},{7,1},{8,14},{10,12},{12... | collective-permute-start | bytes 98312 | tf_op jit(solution)/shard_map/ppermute | solution.py:238
  15.8 1.5 %collective-permute-start.5 = (f32[64,128]{1,0:T(8,128)S(1)}, f32[64,128]{1,0:T(8,128)S(1)}, u32[]{:S(2)}, u32[]{:S(2)}) collective-permute-start(f32[64,128]{1,0:T(8,128)S(1)} %add_add_fusion.2), channel_id=1, source_target_pairs={{0,4},{2,6},{4,0},{6,2},{1,5},{3,7},{5,1},{7,3},{8,12},{10,14},{12... | collective-permute-start | bytes 98312 | tf_op jit(solution)/shard_map/ppermute | solution.py:238
  17.3 0.0 collective-permute-start.4
  17.3 0.6 %collective-permute-done.6 = f32[64,128]{1,0:T(8,128)S(1)} collective-permute-done((f32[64,128]{1,0:T(8,128)S(1)}, f32[64,128]{1,0:T(8,128)S(1)}, u32[]{:S(2)}, u32[]{:S(2)}) %collective-permute-start.6) | collective-permute-done | bytes 32800 | tf_op jit(solution)/shard_map/ppermute | solution.py:238
  18.0 3.3 %collective-permute-done.5 = f32[64,128]{1,0:T(8,128)S(1)} collective-permute-done((f32[64,128]{1,0:T(8,128)S(1)}, f32[64,128]{1,0:T(8,128)S(1)}, u32[]{:S(2)}, u32[]{:S(2)}) %collective-permute-start.5) | collective-permute-done | bytes 32800 | tf_op jit(solution)/shard_map/ppermute | solution.py:238
  21.3 0.0 collective-permute-done.4
  21.3 5.9 %collective-permute-start.7 = (f32[64,128]{1,0:T(8,128)S(1)}, f32[64,128]{1,0:T(8,128)S(1)}, u32[]{:S(2)}, u32[]{:S(2)}) collective-permute-start(f32[64,128]{1,0:T(8,128)S(1)} %add_add_fusion.1), channel_id=1, source_target_pairs={{0,56},{8,48},{16,40},{24,32},{32,24},{40,16},{48,8},{56,0},{1,57}... | collective-permute-start | bytes 98312 | tf_op jit(solution)/shard_map/ppermute | solution.py:238
  27.2 1.9 %collective-permute-done.7 = f32[64,128]{1,0:T(8,128)S(1)} collective-permute-done((f32[64,128]{1,0:T(8,128)S(1)}, f32[64,128]{1,0:T(8,128)S(1)}, u32[]{:S(2)}, u32[]{:S(2)}) %collective-permute-start.7) | collective-permute-done | bytes 32800 | tf_op jit(solution)/shard_map/ppermute | solution.py:238
  29.1 2.0 %collective-permute-start.10 = (f32[64,128]{1,0:T(8,128)S(1)}, f32[64,128]{1,0:T(8,128)S(1)}, u32[]{:S(2)}, u32[]{:S(2)}) collective-permute-start(f32[64,128]{1,0:T(8,128)S(1)} %add.48), channel_id=1, source_target_pairs={{0,24},{8,16},{16,8},{24,0},{32,56},{40,48},{48,40},{56,32},{1,25}... | collective-permute-start | bytes 98312 | tf_op jit(solution)/shard_map/ppermute | solution.py:238
  31.1 1.6 %collective-permute-start.9 = (f32[64,128]{1,0:T(8,128)S(1)}, f32[64,128]{1,0:T(8,128)S(1)}, u32[]{:S(2)}, u32[]{:S(2)}) collective-permute-start(f32[64,128]{1,0:T(8,128)S(1)} %add.48), channel_id=1, source_target_pairs={{0,16},{8,24},{16,0},{24,8},{32,48},{40,56},{48,32},{56,40},{1,17}... | collective-permute-start | bytes 98312 | tf_op jit(solution)/shard_map/ppermute | solution.py:238
  32.8 0.9 %tables.1 = (f32[96,128]{1,0:T(8,128)S(1)}, f32[96,128]{1,0:T(8,128)S(1)}) custom-call(f32[6,16]{1,0:T(8,128)} %value_in.1, f32[6,16]{1,0:T(8,128)} %error_in.1, s32[6]{0:T(128)} %order_in.3), custom_call_target="tpu_custom_call" | custom-call | flops 1048576 | bytes 4194304 | tf_op jit(solution)/shard_map/tables/pallas_call | solution.py:290
  33.7 2.2 %collective-permute-done.9 = f32[64,128]{1,0:T(8,128)S(1)} collective-permute-done((f32[64,128]{1,0:T(8,128)S(1)}, f32[64,128]{1,0:T(8,128)S(1)}, u32[]{:S(2)}, u32[]{:S(2)}) %collective-permute-start.9) | collective-permute-done | bytes 32800 | tf_op jit(solution)/shard_map/ppermute | solution.py:238
  35.9 0.7 %collective-permute-done.8 = f32[64,128]{1,0:T(8,128)S(1)} collective-permute-done((f32[64,128]{1,0:T(8,128)S(1)}, f32[64,128]{1,0:T(8,128)S(1)}, u32[]{:S(2)}, u32[]{:S(2)}) %collective-permute-start.8) | collective-permute-done | bytes 32800 | tf_op jit(solution)/shard_map/ppermute | solution.py:238
  36.7 6.6 %analysis.1 = f32[1024,1024]{1,0:T(8,128)} custom-call(f32[64,128]{1,0:T(8,128)S(1)} %add_add_fusion.rows_t_ref, f32[96,128]{1,0:T(8,128)S(1)} %get-tuple-element.10.values, f32[96,128]{1,0:T(8,128)S(1)} %get-tuple-element.11.noises, f32[16,64,1024]{2,1,0:T(8,128)S(1)} %get-tuple-element.12.tile), custom_call_target="tpu_custom_call" | custom-call | tf_op jit(solution)/shard_map/analysis/pallas_call | solution.py:306
  (7 shorter events, 0.0 us)
Async XLA Ops:
  3.2 1.3 %collective-permute-start = (f32[64,128]{1,0:T(8,128)S(1)}, f32[64,128]{1,0:T(8,128)S(1)}, u32[]{:S(2)}, u32[]{:S(2)}) collective-permute-start(f32[64,128]{1,0:T(8,128)S(1)} %get-tuple-element.9), channel_id=1, source_target_pairs={{0,1},{1,0},{2,3},{3,2},{4,5},{5,4},{6,7},{7,6},{8,9},{9,8},{10,11... | collective-permute-start | bytes 98312 | tf_op jit(solution)/shard_map/ppermute | solution.py:238
  4.6 5.1 %collective-permute-start.3 = (f32[64,128]{1,0:T(8,128)S(1)}, f32[64,128]{1,0:T(8,128)S(1)}, u32[]{:S(2)}, u32[]{:S(2)}) collective-permute-start(f32[64,128]{1,0:T(8,128)S(1)} %add.41), channel_id=1, source_target_pairs={{0,192},{64,128},{128,64},{192,0},{1,193},{65,129},{129,65},{193,1... | collective-permute-start | bytes 98312 | tf_op jit(solution)/shard_map/ppermute | solution.py:238
  7.3 5.4 %collective-permute-start.2 = (f32[64,128]{1,0:T(8,128)S(1)}, f32[64,128]{1,0:T(8,128)S(1)}, u32[]{:S(2)}, u32[]{:S(2)}) collective-permute-start(f32[64,128]{1,0:T(8,128)S(1)} %add.41), channel_id=1, source_target_pairs={{0,128},{64,192},{128,0},{192,64},{1,129},{65,193},{129,1},{193,65... | collective-permute-start | bytes 98312 | tf_op jit(solution)/shard_map/ppermute | solution.py:238
  8.3 4.5 %collective-permute-start.1 = (f32[64,128]{1,0:T(8,128)S(1)}, f32[64,128]{1,0:T(8,128)S(1)}, u32[]{:S(2)}, u32[]{:S(2)}) collective-permute-start(f32[64,128]{1,0:T(8,128)S(1)} %add.41), channel_id=1, source_target_pairs={{0,64},{64,0},{128,192},{192,128},{1,65},{65,1},{129,193},{193,129... | collective-permute-start | bytes 98312 | tf_op jit(solution)/shard_map/ppermute | solution.py:238
  12.7 5.2 %collective-permute-start.6 = (f32[64,128]{1,0:T(8,128)S(1)}, f32[64,128]{1,0:T(8,128)S(1)}, u32[]{:S(2)}, u32[]{:S(2)}) collective-permute-start(f32[64,128]{1,0:T(8,128)S(1)} %add_add_fusion.2), channel_id=1, source_target_pairs={{0,6},{2,4},{4,2},{6,0},{1,7},{3,5},{5,3},{7,1},{8,14},{10,12},{12... | collective-permute-start | bytes 98312 | tf_op jit(solution)/shard_map/ppermute | solution.py:238
  15.8 5.4 %collective-permute-start.5 = (f32[64,128]{1,0:T(8,128)S(1)}, f32[64,128]{1,0:T(8,128)S(1)}, u32[]{:S(2)}, u32[]{:S(2)}) collective-permute-start(f32[64,128]{1,0:T(8,128)S(1)} %add_add_fusion.2), channel_id=1, source_target_pairs={{0,4},{2,6},{4,0},{6,2},{1,5},{3,7},{5,1},{7,3},{8,12},{10,14},{12... | collective-permute-start | bytes 98312 | tf_op jit(solution)/shard_map/ppermute | solution.py:238
  17.3 3.9 %collective-permute-start.4 = (f32[64,128]{1,0:T(8,128)S(1)}, f32[64,128]{1,0:T(8,128)S(1)}, u32[]{:S(2)}, u32[]{:S(2)}) collective-permute-start(f32[64,128]{1,0:T(8,128)S(1)} %add_add_fusion.2), channel_id=1, source_target_pairs={{0,2},{2,0},{4,6},{6,4},{1,3},{3,1},{5,7},{7,5},{8,10},{10,8},{12,... | collective-permute-start | bytes 98312 | tf_op jit(solution)/shard_map/ppermute | solution.py:238
  21.3 7.8 %collective-permute-start.7 = (f32[64,128]{1,0:T(8,128)S(1)}, f32[64,128]{1,0:T(8,128)S(1)}, u32[]{:S(2)}, u32[]{:S(2)}) collective-permute-start(f32[64,128]{1,0:T(8,128)S(1)} %add_add_fusion.1), channel_id=1, source_target_pairs={{0,56},{8,48},{16,40},{24,32},{32,24},{40,16},{48,8},{56,0},{1,57}... | collective-permute-start | bytes 98312 | tf_op jit(solution)/shard_map/ppermute | solution.py:238
  29.1 4.5 %collective-permute-start.10 = (f32[64,128]{1,0:T(8,128)S(1)}, f32[64,128]{1,0:T(8,128)S(1)}, u32[]{:S(2)}, u32[]{:S(2)}) collective-permute-start(f32[64,128]{1,0:T(8,128)S(1)} %add.48), channel_id=1, source_target_pairs={{0,24},{8,16},{16,8},{24,0},{32,56},{40,48},{48,40},{56,32},{1,25}... | collective-permute-start | bytes 98312 | tf_op jit(solution)/shard_map/ppermute | solution.py:238
  31.1 4.8 %collective-permute-start.9 = (f32[64,128]{1,0:T(8,128)S(1)}, f32[64,128]{1,0:T(8,128)S(1)}, u32[]{:S(2)}, u32[]{:S(2)}) collective-permute-start(f32[64,128]{1,0:T(8,128)S(1)} %add.48), channel_id=1, source_target_pairs={{0,16},{8,24},{16,0},{24,8},{32,48},{40,56},{48,32},{56,40},{1,17}... | collective-permute-start | bytes 98312 | tf_op jit(solution)/shard_map/ppermute | solution.py:238
  32.8 3.9 %collective-permute-start.8 = (f32[64,128]{1,0:T(8,128)S(1)}, f32[64,128]{1,0:T(8,128)S(1)}, u32[]{:S(2)}, u32[]{:S(2)}) collective-permute-start(f32[64,128]{1,0:T(8,128)S(1)} %add.48), channel_id=1, source_target_pairs={{0,8},{8,0},{16,24},{24,16},{32,40},{40,32},{48,56},{56,48},{1,9},... | collective-permute-start | bytes 98312 | tf_op jit(solution)/shard_map/ppermute | solution.py:238

commit v2 on v1

--- a/solution.py
+++ b/solution.py
@@ -15,11 +15,11 @@
 
 
 def priors_kernel(
-    sizes, place, lon_in, lat_in, offset_in, owners_in, order_in, field,
+    sizes, lon_in, lat_in, offset_in, owners_in, order_in, field,
     rows_t, tile, lon, lat, offset, owners, order, small_sems, sems
 ):
     groups, obs, members, lon_cells, lat_cells, lat_tiles = sizes
-    my_lon, my_lat = place[0], place[1]
+    my_lon, my_lat = lax.axis_index(LON), lax.axis_index("lat")
     sources = (owners_in, order_in, lon_in, lat_in, offset_in)
     targets = (owners, order, lon, lat, offset)
     small = [
@@ -256,8 +256,6 @@
     groups, obs = obs_lon.shape
     sizes = (groups, obs, members, lon_cells, lat_cells, lax.axis_size("lat"))
     count = groups * obs
-    place = jnp.stack([lax.axis_index(LON), lax.axis_index("lat")]).astype(jnp.int32)
-    smem = pl.BlockSpec(memory_space=pltpu.SMEM)
     vmem = pl.BlockSpec(memory_space=pltpu.VMEM)
     hbm = pl.BlockSpec(memory_space=pltpu.HBM)
     tile_shape = (lon_cells, members, lat_cells)
@@ -273,7 +271,7 @@
             jax.ShapeDtypeStruct((members, LANES), jnp.float32),
             jax.ShapeDtypeStruct(tile_shape, jnp.float32),
         ),
-        in_specs=[smem] + [hbm] * 6,
+        in_specs=[hbm] * 6,
         out_specs=(vmem, vmem),
         scratch_shapes=[
             pltpu.SMEM(obs_lon.shape, jnp.int32),
@@ -286,7 +284,7 @@
         ],
         compiler_params=pltpu.CompilerParams(vmem_limit_bytes=10 << 20),
         name="priors",
-    )(place, lon, lat, offset, owner, order, field)
+    )(lon, lat, offset, owner, order, field)
     values, noises = pl.pallas_call(
         functools.partial(table_kernel, sizes),
         out_shape=(jax.ShapeDtypeStruct((count, LANES), jnp.float32),) * 2,

time: 43.3 us -> 42.6 us (0.984)
  Pallas kernels: 10.6 us -> 10.1 us
  starting transfers between devices: 18.3 us -> 17.8 us
    pallas_call x1, Pallas kernels: 3.17 us -> 2.61 us  [body(): pl.pallas_call(functools.partial(priors_kernel, sizes), out_shape=(jax.Sh...]
    ppermute x11, starting transfers between devices: 18.3 us -> 17.8 us  [pairwise_sum(): lax.ppermute(shard, axis, [(i, partner(i)) for i in range(size)])]
where the time goes in v2:
time: 42.6 us; the launch traced here: 42.5 us
  starting transfers between devices  17.8 us (42%)
  waiting for transfers between devices  14.5 us (34%)
  Pallas kernels  10.1 us (24%)
    ppermute x11, starting transfers between devices, pairwise_sum(): lax.ppermute(shard, axis, [(i, partner(i)) for i in range(size)])  17.8 us
    ppermute x11, waiting for transfers between devices, pairwise_sum(): lax.ppermute(shard, axis, [(i, partner(i)) for i in range(size)])  14.5 us
    pallas_call x1, Pallas kernels, body(): pl.pallas_call(functools.partial(analysis_kernel, sizes), out_shape=jax.S...  6.55 us
    pallas_call x1, Pallas kernels, body(): pl.pallas_call(functools.partial(priors_kernel, sizes), out_shape=(jax.Sh...  2.61 us
    pallas_call x1, Pallas kernels, body(): pl.pallas_call(functools.partial(table_kernel, sizes), out_shape=(jax.Sha...  0.9 us
  transfers between devices with their start and end apart: 11, of which 8 were waited for; matrix products, arithmetic and copies ran while one was open for 0% of the time, Pallas kernels for 2%

profile of v2, /device:TPU:32, one launch (start us, length us, event | category | flops | bytes accessed | tf_op | source)
XLA Modules:
  0.0 42.5 jit_solution(16125768869324912188)
XLA Ops:
  0.0 2.6 %priors.1 = (f32[64,128]{1,0:T(8,128)S(1)}, f32[16,64,1024]{2,1,0:T(8,128)S(1)}) custom-call(s32[6,16]{1,0:T(8,128)} %lon_in.1, s32[6,16]{1,0:T(8,128)} %lat_in.1, f32[6,2,16]{2,1,0:T(2,128)} %offset_in.1, s32[6]{0:T(128)} %owners_in.1, s32[6]{0:T(128)} %order_in.3, f32[64,16,1024]{2,1,0:T(8,128)} %field.1), custom_call_target="tpu_custom_call" | custom-call | tf_op jit(solution)/shard_map/priors/pallas_call | solution.py:268
  2.6 0.1 collective-permute-start
  2.7 1.2 %collective-permute-done = f32[64,128]{1,0:T(8,128)S(1)} collective-permute-done((f32[64,128]{1,0:T(8,128)S(1)}, f32[64,128]{1,0:T(8,128)S(1)}, u32[]{:S(2)}, u32[]{:S(2)}) %collective-permute-start) | collective-permute-done | bytes 32800 | tf_op jit(solution)/shard_map/ppermute | solution.py:238
  3.9 2.8 %collective-permute-start.3 = (f32[64,128]{1,0:T(8,128)S(1)}, f32[64,128]{1,0:T(8,128)S(1)}, u32[]{:S(2)}, u32[]{:S(2)}) collective-permute-start(f32[64,128]{1,0:T(8,128)S(1)} %add.33), channel_id=1, source_target_pairs={{0,192},{64,128},{128,64},{192,0},{1,193},{65,129},{129,65},{193,1... | collective-permute-start | bytes 98312 | tf_op jit(solution)/shard_map/ppermute | solution.py:238
  6.7 0.8 %collective-permute-start.2 = (f32[64,128]{1,0:T(8,128)S(1)}, f32[64,128]{1,0:T(8,128)S(1)}, u32[]{:S(2)}, u32[]{:S(2)}) collective-permute-start(f32[64,128]{1,0:T(8,128)S(1)} %add.33), channel_id=1, source_target_pairs={{0,128},{64,192},{128,0},{192,64},{1,129},{65,193},{129,1},{193,65... | collective-permute-start | bytes 98312 | tf_op jit(solution)/shard_map/ppermute | solution.py:238
  7.5 0.5 %collective-permute-start.1 = (f32[64,128]{1,0:T(8,128)S(1)}, f32[64,128]{1,0:T(8,128)S(1)}, u32[]{:S(2)}, u32[]{:S(2)}) collective-permute-start(f32[64,128]{1,0:T(8,128)S(1)} %add.33), channel_id=1, source_target_pairs={{0,64},{64,0},{128,192},{192,128},{1,65},{65,1},{129,193},{193,129... | collective-permute-start | bytes 98312 | tf_op jit(solution)/shard_map/ppermute | solution.py:238
  8.0 1.0 %collective-permute-done.3 = f32[64,128]{1,0:T(8,128)S(1)} collective-permute-done((f32[64,128]{1,0:T(8,128)S(1)}, f32[64,128]{1,0:T(8,128)S(1)}, u32[]{:S(2)}, u32[]{:S(2)}) %collective-permute-start.3) | collective-permute-done | bytes 32800 | tf_op jit(solution)/shard_map/ppermute | solution.py:238
  9.0 3.1 %collective-permute-done.2 = f32[64,128]{1,0:T(8,128)S(1)} collective-permute-done((f32[64,128]{1,0:T(8,128)S(1)}, f32[64,128]{1,0:T(8,128)S(1)}, u32[]{:S(2)}, u32[]{:S(2)}) %collective-permute-start.2) | collective-permute-done | bytes 32800 | tf_op jit(solution)/shard_map/ppermute | solution.py:238
  12.1 0.0 collective-permute-done.1
  12.1 3.1 %collective-permute-start.6 = (f32[64,128]{1,0:T(8,128)S(1)}, f32[64,128]{1,0:T(8,128)S(1)}, u32[]{:S(2)}, u32[]{:S(2)}) collective-permute-start(f32[64,128]{1,0:T(8,128)S(1)} %add_add_fusion.2), channel_id=1, source_target_pairs={{0,6},{2,4},{4,2},{6,0},{1,7},{3,5},{5,3},{7,1},{8,14},{10,12},{12... | collective-permute-start | bytes 98312 | tf_op jit(solution)/shard_map/ppermute | solution.py:238
  15.2 0.6 %collective-permute-start.5 = (f32[64,128]{1,0:T(8,128)S(1)}, f32[64,128]{1,0:T(8,128)S(1)}, u32[]{:S(2)}, u32[]{:S(2)}) collective-permute-start(f32[64,128]{1,0:T(8,128)S(1)} %add_add_fusion.2), channel_id=1, source_target_pairs={{0,4},{2,6},{4,0},{6,2},{1,5},{3,7},{5,1},{7,3},{8,12},{10,14},{12... | collective-permute-start | bytes 98312 | tf_op jit(solution)/shard_map/ppermute | solution.py:238
  15.9 0.5 %collective-permute-start.4 = (f32[64,128]{1,0:T(8,128)S(1)}, f32[64,128]{1,0:T(8,128)S(1)}, u32[]{:S(2)}, u32[]{:S(2)}) collective-permute-start(f32[64,128]{1,0:T(8,128)S(1)} %add_add_fusion.2), channel_id=1, source_target_pairs={{0,2},{2,0},{4,6},{6,4},{1,3},{3,1},{5,7},{7,5},{8,10},{10,8},{12,... | collective-permute-start | bytes 98312 | tf_op jit(solution)/shard_map/ppermute | solution.py:238
  16.3 1.0 %collective-permute-done.6 = f32[64,128]{1,0:T(8,128)S(1)} collective-permute-done((f32[64,128]{1,0:T(8,128)S(1)}, f32[64,128]{1,0:T(8,128)S(1)}, u32[]{:S(2)}, u32[]{:S(2)}) %collective-permute-start.6) | collective-permute-done | bytes 32800 | tf_op jit(solution)/shard_map/ppermute | solution.py:238
  17.3 3.3 %collective-permute-done.5 = f32[64,128]{1,0:T(8,128)S(1)} collective-permute-done((f32[64,128]{1,0:T(8,128)S(1)}, f32[64,128]{1,0:T(8,128)S(1)}, u32[]{:S(2)}, u32[]{:S(2)}) %collective-permute-start.5) | collective-permute-done | bytes 32800 | tf_op jit(solution)/shard_map/ppermute | solution.py:238
  20.6 0.0 collective-permute-done.4
  20.7 5.9 %collective-permute-start.7 = (f32[64,128]{1,0:T(8,128)S(1)}, f32[64,128]{1,0:T(8,128)S(1)}, u32[]{:S(2)}, u32[]{:S(2)}) collective-permute-start(f32[64,128]{1,0:T(8,128)S(1)} %add_add_fusion.1), channel_id=1, source_target_pairs={{0,56},{8,48},{16,40},{24,32},{32,24},{40,16},{48,8},{56,0},{1,57}... | collective-permute-start | bytes 98312 | tf_op jit(solution)/shard_map/ppermute | solution.py:238
  26.6 1.9 %collective-permute-done.7 = f32[64,128]{1,0:T(8,128)S(1)} collective-permute-done((f32[64,128]{1,0:T(8,128)S(1)}, f32[64,128]{1,0:T(8,128)S(1)}, u32[]{:S(2)}, u32[]{:S(2)}) %collective-permute-start.7) | collective-permute-done | bytes 32800 | tf_op jit(solution)/shard_map/ppermute | solution.py:238
  28.5 1.1 %collective-permute-start.10 = (f32[64,128]{1,0:T(8,128)S(1)}, f32[64,128]{1,0:T(8,128)S(1)}, u32[]{:S(2)}, u32[]{:S(2)}) collective-permute-start(f32[64,128]{1,0:T(8,128)S(1)} %add.40), channel_id=1, source_target_pairs={{0,24},{8,16},{16,8},{24,0},{32,56},{40,48},{48,40},{56,32},{1,25}... | collective-permute-start | bytes 98312 | tf_op jit(solution)/shard_map/ppermute | solution.py:238
  29.6 2.4 %collective-permute-start.9 = (f32[64,128]{1,0:T(8,128)S(1)}, f32[64,128]{1,0:T(8,128)S(1)}, u32[]{:S(2)}, u32[]{:S(2)}) collective-permute-start(f32[64,128]{1,0:T(8,128)S(1)} %add.40), channel_id=1, source_target_pairs={{0,16},{8,24},{16,0},{24,8},{32,48},{40,56},{48,32},{56,40},{1,17}... | collective-permute-start | bytes 98312 | tf_op jit(solution)/shard_map/ppermute | solution.py:238
  32.0 0.0 collective-permute-start.8
  32.0 0.9 %tables.1 = (f32[96,128]{1,0:T(8,128)S(1)}, f32[96,128]{1,0:T(8,128)S(1)}) custom-call(f32[6,16]{1,0:T(8,128)} %value_in.1, f32[6,16]{1,0:T(8,128)} %error_in.1, s32[6]{0:T(128)} %order_in.3), custom_call_target="tpu_custom_call" | custom-call | flops 1048576 | bytes 4194304 | tf_op jit(solution)/shard_map/tables/pallas_call | solution.py:288
  33.0 1.5 %collective-permute-done.9 = f32[64,128]{1,0:T(8,128)S(1)} collective-permute-done((f32[64,128]{1,0:T(8,128)S(1)}, f32[64,128]{1,0:T(8,128)S(1)}, u32[]{:S(2)}, u32[]{:S(2)}) %collective-permute-start.9) | collective-permute-done | bytes 32800 | tf_op jit(solution)/shard_map/ppermute | solution.py:238
  34.4 1.5 %collective-permute-done.8 = f32[64,128]{1,0:T(8,128)S(1)} collective-permute-done((f32[64,128]{1,0:T(8,128)S(1)}, f32[64,128]{1,0:T(8,128)S(1)}, u32[]{:S(2)}, u32[]{:S(2)}) %collective-permute-start.8) | collective-permute-done | bytes 32800 | tf_op jit(solution)/shard_map/ppermute | solution.py:238
  36.0 6.6 %analysis.1 = f32[1024,1024]{1,0:T(8,128)} custom-call(f32[64,128]{1,0:T(8,128)S(1)} %add_add_fusion.rows_t_ref, f32[96,128]{1,0:T(8,128)S(1)} %get-tuple-element.10.values, f32[96,128]{1,0:T(8,128)S(1)} %get-tuple-element.11.noises, f32[16,64,1024]{2,1,0:T(8,128)S(1)} %get-tuple-element.12.tile), custom_call_target="tpu_custom_call" | custom-call | tf_op jit(solution)/shard_map/analysis/pallas_call | solution.py:304
  (6 shorter events, 0.0 us)
Async XLA Ops:
  2.6 1.3 %collective-permute-start = (f32[64,128]{1,0:T(8,128)S(1)}, f32[64,128]{1,0:T(8,128)S(1)}, u32[]{:S(2)}, u32[]{:S(2)}) collective-permute-start(f32[64,128]{1,0:T(8,128)S(1)} %get-tuple-element.9), channel_id=1, source_target_pairs={{0,1},{1,0},{2,3},{3,2},{4,5},{5,4},{6,7},{7,6},{8,9},{9,8},{10,11... | collective-permute-start | bytes 98312 | tf_op jit(solution)/shard_map/ppermute | solution.py:238
  3.9 5.1 %collective-permute-start.3 = (f32[64,128]{1,0:T(8,128)S(1)}, f32[64,128]{1,0:T(8,128)S(1)}, u32[]{:S(2)}, u32[]{:S(2)}) collective-permute-start(f32[64,128]{1,0:T(8,128)S(1)} %add.33), channel_id=1, source_target_pairs={{0,192},{64,128},{128,64},{192,0},{1,193},{65,129},{129,65},{193,1... | collective-permute-start | bytes 98312 | tf_op jit(solution)/shard_map/ppermute | solution.py:238
  6.7 5.4 %collective-permute-start.2 = (f32[64,128]{1,0:T(8,128)S(1)}, f32[64,128]{1,0:T(8,128)S(1)}, u32[]{:S(2)}, u32[]{:S(2)}) collective-permute-start(f32[64,128]{1,0:T(8,128)S(1)} %add.33), channel_id=1, source_target_pairs={{0,128},{64,192},{128,0},{192,64},{1,129},{65,193},{129,1},{193,65... | collective-permute-start | bytes 98312 | tf_op jit(solution)/shard_map/ppermute | solution.py:238
  7.5 4.6 %collective-permute-start.1 = (f32[64,128]{1,0:T(8,128)S(1)}, f32[64,128]{1,0:T(8,128)S(1)}, u32[]{:S(2)}, u32[]{:S(2)}) collective-permute-start(f32[64,128]{1,0:T(8,128)S(1)} %add.33), channel_id=1, source_target_pairs={{0,64},{64,0},{128,192},{192,128},{1,65},{65,1},{129,193},{193,129... | collective-permute-start | bytes 98312 | tf_op jit(solution)/shard_map/ppermute | solution.py:238
  12.1 5.2 %collective-permute-start.6 = (f32[64,128]{1,0:T(8,128)S(1)}, f32[64,128]{1,0:T(8,128)S(1)}, u32[]{:S(2)}, u32[]{:S(2)}) collective-permute-start(f32[64,128]{1,0:T(8,128)S(1)} %add_add_fusion.2), channel_id=1, source_target_pairs={{0,6},{2,4},{4,2},{6,0},{1,7},{3,5},{5,3},{7,1},{8,14},{10,12},{12... | collective-permute-start | bytes 98312 | tf_op jit(solution)/shard_map/ppermute | solution.py:238
  15.2 5.4 %collective-permute-start.5 = (f32[64,128]{1,0:T(8,128)S(1)}, f32[64,128]{1,0:T(8,128)S(1)}, u32[]{:S(2)}, u32[]{:S(2)}) collective-permute-start(f32[64,128]{1,0:T(8,128)S(1)} %add_add_fusion.2), channel_id=1, source_target_pairs={{0,4},{2,6},{4,0},{6,2},{1,5},{3,7},{5,1},{7,3},{8,12},{10,14},{12... | collective-permute-start | bytes 98312 | tf_op jit(solution)/shard_map/ppermute | solution.py:238
  15.9 4.8 %collective-permute-start.4 = (f32[64,128]{1,0:T(8,128)S(1)}, f32[64,128]{1,0:T(8,128)S(1)}, u32[]{:S(2)}, u32[]{:S(2)}) collective-permute-start(f32[64,128]{1,0:T(8,128)S(1)} %add_add_fusion.2), channel_id=1, source_target_pairs={{0,2},{2,0},{4,6},{6,4},{1,3},{3,1},{5,7},{7,5},{8,10},{10,8},{12,... | collective-permute-start | bytes 98312 | tf_op jit(solution)/shard_map/ppermute | solution.py:238
  20.7 7.8 %collective-permute-start.7 = (f32[64,128]{1,0:T(8,128)S(1)}, f32[64,128]{1,0:T(8,128)S(1)}, u32[]{:S(2)}, u32[]{:S(2)}) collective-permute-start(f32[64,128]{1,0:T(8,128)S(1)} %add_add_fusion.1), channel_id=1, source_target_pairs={{0,56},{8,48},{16,40},{24,32},{32,24},{40,16},{48,8},{56,0},{1,57}... | collective-permute-start | bytes 98312 | tf_op jit(solution)/shard_map/ppermute | solution.py:238
  28.5 4.5 %collective-permute-start.10 = (f32[64,128]{1,0:T(8,128)S(1)}, f32[64,128]{1,0:T(8,128)S(1)}, u32[]{:S(2)}, u32[]{:S(2)}) collective-permute-start(f32[64,128]{1,0:T(8,128)S(1)} %add.40), channel_id=1, source_target_pairs={{0,24},{8,16},{16,8},{24,0},{32,56},{40,48},{48,40},{56,32},{1,25}... | collective-permute-start | bytes 98312 | tf_op jit(solution)/shard_map/ppermute | solution.py:238
  29.6 4.8 %collective-permute-start.9 = (f32[64,128]{1,0:T(8,128)S(1)}, f32[64,128]{1,0:T(8,128)S(1)}, u32[]{:S(2)}, u32[]{:S(2)}) collective-permute-start(f32[64,128]{1,0:T(8,128)S(1)} %add.40), channel_id=1, source_target_pairs={{0,16},{8,24},{16,0},{24,8},{32,48},{40,56},{48,32},{56,40},{1,17}... | collective-permute-start | bytes 98312 | tf_op jit(solution)/shard_map/ppermute | solution.py:238
  32.0 3.9 %collective-permute-start.8 = (f32[64,128]{1,0:T(8,128)S(1)}, f32[64,128]{1,0:T(8,128)S(1)}, u32[]{:S(2)}, u32[]{:S(2)}) collective-permute-start(f32[64,128]{1,0:T(8,128)S(1)} %add.40), channel_id=1, source_target_pairs={{0,8},{8,0},{16,24},{24,16},{32,40},{40,32},{48,56},{56,48},{1,9},... | collective-permute-start | bytes 98312 | tf_op jit(solution)/shard_map/ppermute | solution.py:238

commit v3 on v2

--- a/solution.py
+++ b/solution.py
@@ -77,7 +77,17 @@
                             row = jnp.clip(row, 0, lon_cells - 1)
                             total = total + tile[row, :, pl.ds(start, LANES)] * (lat_hat * hat)
                         found = jnp.sum(total, axis=1, keepdims=True)
-                        rows_t[...] += jnp.where(lane == turn * obs + k, found, 0.0)
+                        index = turn * obs + k
+                        wide = jnp.where(index < 64, index, 1000)
+                        narrow = jnp.where(index < 64, -1000, index - 64)
+                        rows_t[0:32, :] += jnp.where(lane == wide, found[0:32], 0.0) + jnp.where(
+                            lane == wide + 64, found[32:64], 0.0
+                        )
+                        tail = jnp.zeros((16, LANES), jnp.float32)
+                        for q4 in range(4):
+                            piece = found[q4 * 16 : q4 * 16 + 16]
+                            tail = jnp.where(lane == narrow + q4 * 32, piece, tail)
+                        rows_t[32:48, :] += tail
 
                     share(first)
 
@@ -116,7 +126,14 @@
 ):
     groups, obs, members, lon_cells, lat_cells, lat_tiles = sizes
     count = groups * obs
-    priors = rows_t_ref[...]
+    packed = rows_t_ref[0:32, :]
+    early = jnp.concatenate([packed, pltpu.roll(packed, 64, 1)], axis=0)
+    tail = rows_t_ref[32:48, :]
+    late = jnp.concatenate(
+        [tail if n == 2 else pltpu.roll(tail, (64 - 32 * n) % LANES, 1) for n in range(4)], axis=0
+    )
+    at = lax.broadcasted_iota(jnp.int32, (members, LANES), 1)
+    priors = jnp.where(at < 64, early, jnp.where(at < groups * obs, late, 0.0))
     mean = jnp.mean(priors, axis=0, keepdims=True)
     anomalies = priors - mean
     eye = (
@@ -268,7 +285,7 @@
     rows_t, tile = pl.pallas_call(
         functools.partial(priors_kernel, sizes),
         out_shape=(
-            jax.ShapeDtypeStruct((members, LANES), jnp.float32),
+            jax.ShapeDtypeStruct((count * members // LANES, LANES), jnp.float32),
             jax.ShapeDtypeStruct(tile_shape, jnp.float32),
         ),
         in_specs=[hbm] * 6,

time: 42.6 us -> 43 us (level)
  starting transfers between devices: 17.8 us -> 19.8 us
  waiting for transfers between devices: 14.5 us -> 12.8 us
    ppermute x11, starting transfers between devices: 17.8 us -> 19.8 us  [pairwise_sum(): lax.ppermute(shard, axis, [(i, partner(i)) for i in range(size)])]
    ppermute x11, waiting for transfers between devices: 14.5 us -> 12.8 us  [pairwise_sum(): lax.ppermute(shard, axis, [(i, partner(i)) for i in range(size)])]
where the time goes in v3:
time: 43 us; the launch traced here: 42.7 us
  starting transfers between devices  19.8 us (46%)
  waiting for transfers between devices  12.8 us (30%)
  Pallas kernels  10.1 us (23%)
    ppermute x11, starting transfers between devices, pairwise_sum(): lax.ppermute(shard, axis, [(i, partner(i)) for i in range(size)])  19.8 us
    ppermute x11, waiting for transfers between devices, pairwise_sum(): lax.ppermute(shard, axis, [(i, partner(i)) for i in range(size)])  12.8 us
    pallas_call x1, Pallas kernels, body(): pl.pallas_call(functools.partial(analysis_kernel, sizes), out_shape=jax.S...  6.62 us
    pallas_call x1, Pallas kernels, body(): pl.pallas_call(functools.partial(priors_kernel, sizes), out_shape=(jax.Sh...  2.61 us
    pallas_call x1, Pallas kernels, body(): pl.pallas_call(functools.partial(table_kernel, sizes), out_shape=(jax.Sha...  0.9 us
  transfers between devices with their start and end apart: 11, of which 8 were waited for; matrix products, arithmetic and copies ran while one was open for 0% of the time, Pallas kernels for 2%

profile of v3, /device:TPU:32, one launch (start us, length us, event | category | flops | bytes accessed | tf_op | source)
XLA Modules:
  0.0 42.7 jit_solution(13689547860571946670)
XLA Ops:
  0.0 2.6 %priors.1 = (f32[48,128]{1,0:T(8,128)S(1)}, f32[16,64,1024]{2,1,0:T(8,128)S(1)}) custom-call(s32[6,16]{1,0:T(8,128)} %lon_in.1, s32[6,16]{1,0:T(8,128)} %lat_in.1, f32[6,2,16]{2,1,0:T(2,128)} %offset_in.1, s32[6]{0:T(128)} %owners_in.1, s32[6]{0:T(128)} %order_in.3, f32[64,16,1024]{2,1,0:T(8,128)} %field.1), custom_call_target="tpu_custom_call" | custom-call | tf_op jit(solution)/shard_map/priors/pallas_call | solution.py:285
  2.6 0.1 collective-permute-start
  2.7 1.2 %collective-permute-done = f32[48,128]{1,0:T(8,128)S(1)} collective-permute-done((f32[48,128]{1,0:T(8,128)S(1)}, f32[48,128]{1,0:T(8,128)S(1)}, u32[]{:S(2)}, u32[]{:S(2)}) %collective-permute-start) | collective-permute-done | bytes 24608 | tf_op jit(solution)/shard_map/ppermute | solution.py:255
  3.9 2.8 %collective-permute-start.3 = (f32[48,128]{1,0:T(8,128)S(1)}, f32[48,128]{1,0:T(8,128)S(1)}, u32[]{:S(2)}, u32[]{:S(2)}) collective-permute-start(f32[48,128]{1,0:T(8,128)S(1)} %add.33), channel_id=1, source_target_pairs={{0,192},{64,128},{128,64},{192,0},{1,193},{65,129},{129,65},{193,1... | collective-permute-start | bytes 73736 | tf_op jit(solution)/shard_map/ppermute | solution.py:255
  6.7 0.8 %collective-permute-start.2 = (f32[48,128]{1,0:T(8,128)S(1)}, f32[48,128]{1,0:T(8,128)S(1)}, u32[]{:S(2)}, u32[]{:S(2)}) collective-permute-start(f32[48,128]{1,0:T(8,128)S(1)} %add.33), channel_id=1, source_target_pairs={{0,128},{64,192},{128,0},{192,64},{1,129},{65,193},{129,1},{193,65... | collective-permute-start | bytes 73736 | tf_op jit(solution)/shard_map/ppermute | solution.py:255
  7.5 0.5 %collective-permute-start.1 = (f32[48,128]{1,0:T(8,128)S(1)}, f32[48,128]{1,0:T(8,128)S(1)}, u32[]{:S(2)}, u32[]{:S(2)}) collective-permute-start(f32[48,128]{1,0:T(8,128)S(1)} %add.33), channel_id=1, source_target_pairs={{0,64},{64,0},{128,192},{192,128},{1,65},{65,1},{129,193},{193,129... | collective-permute-start | bytes 73736 | tf_op jit(solution)/shard_map/ppermute | solution.py:255
  8.0 0.9 %collective-permute-done.3 = f32[48,128]{1,0:T(8,128)S(1)} collective-permute-done((f32[48,128]{1,0:T(8,128)S(1)}, f32[48,128]{1,0:T(8,128)S(1)}, u32[]{:S(2)}, u32[]{:S(2)}) %collective-permute-start.3) | collective-permute-done | bytes 24608 | tf_op jit(solution)/shard_map/ppermute | solution.py:255
  8.9 3.1 %collective-permute-done.2 = f32[48,128]{1,0:T(8,128)S(1)} collective-permute-done((f32[48,128]{1,0:T(8,128)S(1)}, f32[48,128]{1,0:T(8,128)S(1)}, u32[]{:S(2)}, u32[]{:S(2)}) %collective-permute-start.2) | collective-permute-done | bytes 24608 | tf_op jit(solution)/shard_map/ppermute | solution.py:255
  12.0 0.0 collective-permute-done.1
  12.0 3.1 %collective-permute-start.6 = (f32[48,128]{1,0:T(8,128)S(1)}, f32[48,128]{1,0:T(8,128)S(1)}, u32[]{:S(2)}, u32[]{:S(2)}) collective-permute-start(f32[48,128]{1,0:T(8,128)S(1)} %add_add_fusion.2), channel_id=1, source_target_pairs={{0,6},{2,4},{4,2},{6,0},{1,7},{3,5},{5,3},{7,1},{8,14},{10,12},{12... | collective-permute-start | bytes 73736 | tf_op jit(solution)/shard_map/ppermute | solution.py:255
  15.1 0.6 %collective-permute-start.5 = (f32[48,128]{1,0:T(8,128)S(1)}, f32[48,128]{1,0:T(8,128)S(1)}, u32[]{:S(2)}, u32[]{:S(2)}) collective-permute-start(f32[48,128]{1,0:T(8,128)S(1)} %add_add_fusion.2), channel_id=1, source_target_pairs={{0,4},{2,6},{4,0},{6,2},{1,5},{3,7},{5,1},{7,3},{8,12},{10,14},{12... | collective-permute-start | bytes 73736 | tf_op jit(solution)/shard_map/ppermute | solution.py:255
  15.7 0.5 %collective-permute-start.4 = (f32[48,128]{1,0:T(8,128)S(1)}, f32[48,128]{1,0:T(8,128)S(1)}, u32[]{:S(2)}, u32[]{:S(2)}) collective-permute-start(f32[48,128]{1,0:T(8,128)S(1)} %add_add_fusion.2), channel_id=1, source_target_pairs={{0,2},{2,0},{4,6},{6,4},{1,3},{3,1},{5,7},{7,5},{8,10},{10,8},{12,... | collective-permute-start | bytes 73736 | tf_op jit(solution)/shard_map/ppermute | solution.py:255
  16.2 0.9 %collective-permute-done.6 = f32[48,128]{1,0:T(8,128)S(1)} collective-permute-done((f32[48,128]{1,0:T(8,128)S(1)}, f32[48,128]{1,0:T(8,128)S(1)}, u32[]{:S(2)}, u32[]{:S(2)}) %collective-permute-start.6) | collective-permute-done | bytes 24608 | tf_op jit(solution)/shard_map/ppermute | solution.py:255
  17.1 3.3 %collective-permute-done.5 = f32[48,128]{1,0:T(8,128)S(1)} collective-permute-done((f32[48,128]{1,0:T(8,128)S(1)}, f32[48,128]{1,0:T(8,128)S(1)}, u32[]{:S(2)}, u32[]{:S(2)}) %collective-permute-start.5) | collective-permute-done | bytes 24608 | tf_op jit(solution)/shard_map/ppermute | solution.py:255
  20.4 0.0 collective-permute-done.4
  20.5 7.9 %collective-permute-start.7 = (f32[48,128]{1,0:T(8,128)S(1)}, f32[48,128]{1,0:T(8,128)S(1)}, u32[]{:S(2)}, u32[]{:S(2)}) collective-permute-start(f32[48,128]{1,0:T(8,128)S(1)} %add_add_fusion.1), channel_id=1, source_target_pairs={{0,56},{8,48},{16,40},{24,32},{32,24},{40,16},{48,8},{56,0},{1,57}... | collective-permute-start | bytes 73736 | tf_op jit(solution)/shard_map/ppermute | solution.py:255
  28.4 1.8 %collective-permute-done.7 = f32[48,128]{1,0:T(8,128)S(1)} collective-permute-done((f32[48,128]{1,0:T(8,128)S(1)}, f32[48,128]{1,0:T(8,128)S(1)}, u32[]{:S(2)}, u32[]{:S(2)}) %collective-permute-start.7) | collective-permute-done | bytes 24608 | tf_op jit(solution)/shard_map/ppermute | solution.py:255
  30.2 0.4 collective-permute-start.10
  30.6 1.7 %collective-permute-start.9 = (f32[48,128]{1,0:T(8,128)S(1)}, f32[48,128]{1,0:T(8,128)S(1)}, u32[]{:S(2)}, u32[]{:S(2)}) collective-permute-start(f32[48,128]{1,0:T(8,128)S(1)} %add.40), channel_id=1, source_target_pairs={{0,16},{8,24},{16,0},{24,8},{32,48},{40,56},{48,32},{56,40},{1,17}... | collective-permute-start | bytes 73736 | tf_op jit(solution)/shard_map/ppermute | solution.py:255
  32.3 1.4 %collective-permute-start.8 = (f32[48,128]{1,0:T(8,128)S(1)}, f32[48,128]{1,0:T(8,128)S(1)}, u32[]{:S(2)}, u32[]{:S(2)}) collective-permute-start(f32[48,128]{1,0:T(8,128)S(1)} %add.40), channel_id=1, source_target_pairs={{0,8},{8,0},{16,24},{24,16},{32,40},{40,32},{48,56},{56,48},{1,9},... | collective-permute-start | bytes 73736 | tf_op jit(solution)/shard_map/ppermute | solution.py:255
  33.7 0.9 %tables.1 = (f32[96,128]{1,0:T(8,128)S(1)}, f32[96,128]{1,0:T(8,128)S(1)}) custom-call(f32[6,16]{1,0:T(8,128)} %value_in.1, f32[6,16]{1,0:T(8,128)} %error_in.1, s32[6]{0:T(128)} %order_in.3), custom_call_target="tpu_custom_call" | custom-call | flops 1048576 | bytes 4194304 | tf_op jit(solution)/shard_map/tables/pallas_call | solution.py:305
  34.6 0.7 %collective-permute-done.9 = f32[48,128]{1,0:T(8,128)S(1)} collective-permute-done((f32[48,128]{1,0:T(8,128)S(1)}, f32[48,128]{1,0:T(8,128)S(1)}, u32[]{:S(2)}, u32[]{:S(2)}) %collective-permute-start.9) | collective-permute-done | bytes 24608 | tf_op jit(solution)/shard_map/ppermute | solution.py:255
  35.3 0.8 %collective-permute-done.8 = f32[48,128]{1,0:T(8,128)S(1)} collective-permute-done((f32[48,128]{1,0:T(8,128)S(1)}, f32[48,128]{1,0:T(8,128)S(1)}, u32[]{:S(2)}, u32[]{:S(2)}) %collective-permute-start.8) | collective-permute-done | bytes 24608 | tf_op jit(solution)/shard_map/ppermute | solution.py:255
  36.1 6.6 %analysis.1 = f32[1024,1024]{1,0:T(8,128)} custom-call(f32[48,128]{1,0:T(8,128)S(1)} %add_add_fusion.rows_t_ref, f32[96,128]{1,0:T(8,128)S(1)} %get-tuple-element.10.values, f32[96,128]{1,0:T(8,128)S(1)} %get-tuple-element.11.noises, f32[16,64,1024]{2,1,0:T(8,128)S(1)} %get-tuple-element.12.tile), custom_call_target="tpu_custom_call" | custom-call | tf_op jit(solution)/shard_map/analysis/pallas_call | solution.py:321
  (6 shorter events, 0.0 us)
Async XLA Ops:
  2.6 1.3 %collective-permute-start = (f32[48,128]{1,0:T(8,128)S(1)}, f32[48,128]{1,0:T(8,128)S(1)}, u32[]{:S(2)}, u32[]{:S(2)}) collective-permute-start(f32[48,128]{1,0:T(8,128)S(1)} %get-tuple-element.9), channel_id=1, source_target_pairs={{0,1},{1,0},{2,3},{3,2},{4,5},{5,4},{6,7},{7,6},{8,9},{9,8},{10,11... | collective-permute-start | bytes 73736 | tf_op jit(solution)/shard_map/ppermute | solution.py:255
  3.9 5.0 %collective-permute-start.3 = (f32[48,128]{1,0:T(8,128)S(1)}, f32[48,128]{1,0:T(8,128)S(1)}, u32[]{:S(2)}, u32[]{:S(2)}) collective-permute-start(f32[48,128]{1,0:T(8,128)S(1)} %add.33), channel_id=1, source_target_pairs={{0,192},{64,128},{128,64},{192,0},{1,193},{65,129},{129,65},{193,1... | collective-permute-start | bytes 73736 | tf_op jit(solution)/shard_map/ppermute | solution.py:255
  6.7 5.3 %collective-permute-start.2 = (f32[48,128]{1,0:T(8,128)S(1)}, f32[48,128]{1,0:T(8,128)S(1)}, u32[]{:S(2)}, u32[]{:S(2)}) collective-permute-start(f32[48,128]{1,0:T(8,128)S(1)} %add.33), channel_id=1, source_target_pairs={{0,128},{64,192},{128,0},{192,64},{1,129},{65,193},{129,1},{193,65... | collective-permute-start | bytes 73736 | tf_op jit(solution)/shard_map/ppermute | solution.py:255
  7.5 4.5 %collective-permute-start.1 = (f32[48,128]{1,0:T(8,128)S(1)}, f32[48,128]{1,0:T(8,128)S(1)}, u32[]{:S(2)}, u32[]{:S(2)}) collective-permute-start(f32[48,128]{1,0:T(8,128)S(1)} %add.33), channel_id=1, source_target_pairs={{0,64},{64,0},{128,192},{192,128},{1,65},{65,1},{129,193},{193,129... | collective-permute-start | bytes 73736 | tf_op jit(solution)/shard_map/ppermute | solution.py:255
  12.0 5.1 %collective-permute-start.6 = (f32[48,128]{1,0:T(8,128)S(1)}, f32[48,128]{1,0:T(8,128)S(1)}, u32[]{:S(2)}, u32[]{:S(2)}) collective-permute-start(f32[48,128]{1,0:T(8,128)S(1)} %add_add_fusion.2), channel_id=1, source_target_pairs={{0,6},{2,4},{4,2},{6,0},{1,7},{3,5},{5,3},{7,1},{8,14},{10,12},{12... | collective-permute-start | bytes 73736 | tf_op jit(solution)/shard_map/ppermute | solution.py:255
  15.1 5.3 %collective-permute-start.5 = (f32[48,128]{1,0:T(8,128)S(1)}, f32[48,128]{1,0:T(8,128)S(1)}, u32[]{:S(2)}, u32[]{:S(2)}) collective-permute-start(f32[48,128]{1,0:T(8,128)S(1)} %add_add_fusion.2), channel_id=1, source_target_pairs={{0,4},{2,6},{4,0},{6,2},{1,5},{3,7},{5,1},{7,3},{8,12},{10,14},{12... | collective-permute-start | bytes 73736 | tf_op jit(solution)/shard_map/ppermute | solution.py:255
  15.7 4.7 %collective-permute-start.4 = (f32[48,128]{1,0:T(8,128)S(1)}, f32[48,128]{1,0:T(8,128)S(1)}, u32[]{:S(2)}, u32[]{:S(2)}) collective-permute-start(f32[48,128]{1,0:T(8,128)S(1)} %add_add_fusion.2), channel_id=1, source_target_pairs={{0,2},{2,0},{4,6},{6,4},{1,3},{3,1},{5,7},{7,5},{8,10},{10,8},{12,... | collective-permute-start | bytes 73736 | tf_op jit(solution)/shard_map/ppermute | solution.py:255
  20.5 9.7 %collective-permute-start.7 = (f32[48,128]{1,0:T(8,128)S(1)}, f32[48,128]{1,0:T(8,128)S(1)}, u32[]{:S(2)}, u32[]{:S(2)}) collective-permute-start(f32[48,128]{1,0:T(8,128)S(1)} %add_add_fusion.1), channel_id=1, source_target_pairs={{0,56},{8,48},{16,40},{24,32},{32,24},{40,16},{48,8},{56,0},{1,57}... | collective-permute-start | bytes 73736 | tf_op jit(solution)/shard_map/ppermute | solution.py:255
  30.2 4.4 %collective-permute-start.10 = (f32[48,128]{1,0:T(8,128)S(1)}, f32[48,128]{1,0:T(8,128)S(1)}, u32[]{:S(2)}, u32[]{:S(2)}) collective-permute-start(f32[48,128]{1,0:T(8,128)S(1)} %add.40), channel_id=1, source_target_pairs={{0,24},{8,16},{16,8},{24,0},{32,56},{40,48},{48,40},{56,32},{1,25}... | collective-permute-start | bytes 73736 | tf_op jit(solution)/shard_map/ppermute | solution.py:255
  30.6 4.7 %collective-permute-start.9 = (f32[48,128]{1,0:T(8,128)S(1)}, f32[48,128]{1,0:T(8,128)S(1)}, u32[]{:S(2)}, u32[]{:S(2)}) collective-permute-start(f32[48,128]{1,0:T(8,128)S(1)} %add.40), channel_id=1, source_target_pairs={{0,16},{8,24},{16,0},{24,8},{32,48},{40,56},{48,32},{56,40},{1,17}... | collective-permute-start | bytes 73736 | tf_op jit(solution)/shard_map/ppermute | solution.py:255
  32.3 3.8 %collective-permute-start.8 = (f32[48,128]{1,0:T(8,128)S(1)}, f32[48,128]{1,0:T(8,128)S(1)}, u32[]{:S(2)}, u32[]{:S(2)}) collective-permute-start(f32[48,128]{1,0:T(8,128)S(1)} %add.40), channel_id=1, source_target_pairs={{0,8},{8,0},{16,24},{24,16},{32,40},{40,32},{48,56},{56,48},{1,9},... | collective-permute-start | bytes 73736 | tf_op jit(solution)/shard_map/ppermute | solution.py:255
